TPU v7x, 32 devices: a whole 2x2x4 slice. The times are simulated.
32 devices in a mesh: dp: 8 (over z, x), seq: 4 (over y, core).
Axes of the slice: x: 2, y: 2, z: 4, core: 2. Of those that a mesh axis runs over, the one named last changes fastest.
Arguments:
- query: bfloat16 [8, 1024, 2048], P('dp', 'seq'), may hold values from -6 to 6
- keys: bfloat16 [8, 1024, 256], P('dp', 'seq'), may hold values from -6 to 6
- values: bfloat16 [8, 1024, 256], P('dp', 'seq'), may hold values from -6 to 6
- grad_out: bfloat16 [8, 1024, 2048], P('dp', 'seq'), may hold values from -6 to 6
- layer_input: bfloat16 [8, 1024, 1536], P('dp', 'seq'), may hold values from -6 to 6
- sinks: float32 [32], replicated, may hold values from 1 to 5
- segments: int32 [8, 1024], P('dp', 'seq'), may hold values from 0 to 255, as said below
- positions: int32 [8, 1024], P('dp', 'seq'), may hold values from 0 to 8191, as said below
Outputs:
- grad_query: bfloat16 [8, 1024, 2048], P('dp', 'seq')
- weight_grads: float32 [1536, 256], P('dp')
Inputs may be any that keep to these rules, and one draw needn't show every extreme that they name: `segments`: segment ids never fall along a span. positions rise by one inside a document.
All inputs are finite; a program needn't handle non-finite values.
Results may differ from a plain program's by a relative error of at most 0.0086.
Values may be sent and summed in bfloat16 or wider, within the bound.
No kernel may reach another device: no remote copies, remote signals or barrier semaphores. Data moves between devices by JAX's collectives and lax.ppermute only.
A program may use at most 64 MiB of HBM per device.

v0:
```python
import jax
import jax.numpy as jnp
from jax import lax
from jax.sharding import PartitionSpec as P

HEADDIM = 64
WINDOW = 128
theta_base = 150000.0
seg_modulus = 256


def from_behind(shard, axis, by):
    count = lax.axis_size(axis)
    pairs = [(i, i + by) for i in range(count) if 0 <= i + by < count]
    return lax.ppermute(shard, axis, pairs)


def rotate_back(grads, token_pos):
    half_dim = grads.shape[-1] // 2
    frequency = theta_base ** (-(jnp.arange(half_dim, dtype=jnp.float32) * 2.0 / grads.shape[-1]))
    angles = token_pos.astype(jnp.float32)[:, None] * frequency[None, :]
    cosine = jnp.cos(angles)[:, None, :]
    sine_val = jnp.sin(angles)[:, None, :]
    lower_half = grads[..., :half_dim]
    upper_half = grads[..., half_dim:]
    return jnp.concatenate(
        [lower_half * cosine + upper_half * sine_val, upper_half * cosine - lower_half * sine_val],
        axis=-1,
    )


def body(query, keys, values, grad_out, layer_input, sinks, segments, positions):
    query = query[0]
    keys = keys[0]
    values = values[0]
    grad_out = grad_out[0]
    layer_input = layer_input[0]
    segments = segments[0]
    positions = positions[0]
    tok_rows = query.shape[0]
    head_dim = HEADDIM
    heads_q = sinks.shape[0]
    heads_kv = keys.shape[1] // head_dim
    group = heads_q // heads_kv
    width = WINDOW
    scale = 1.0 / head_dim**0.5
    seg_local = jnp.remainder(segments, seg_modulus).astype(jnp.float32)
    rim_keys, rim_values, rim_segs = from_behind(
        (
            keys[tok_rows - width :],
            values[tok_rows - width :],
            seg_local[tok_rows - width :].astype(jnp.bfloat16),
        ),
        "seq",
        1,
    )
    all_keys = jnp.concatenate([rim_keys, keys], axis=0)
    all_values = jnp.concatenate([rim_values, values], axis=0)
    key_segs = jnp.concatenate([rim_segs.astype(jnp.float32), seg_local], axis=0)
    seq_index = lax.axis_index("seq")
    query_idx = jnp.arange(tok_rows)[:, None] + width
    key_idx = jnp.arange(tok_rows + width)[None, :]
    offset = query_idx - key_idx
    allowed = (offset >= 0) & (offset < width) & (seg_local[:, None] == key_segs[None, :])
    allowed = allowed & ((key_idx >= width) | (seq_index > 0))
    allowed = allowed[None]
    query_parts = []
    key_parts = []
    for head_group in range(heads_kv):
        low_col = head_group * group * head_dim
        high_col = low_col + group * head_dim
        q_grp = query[:, low_col:high_col].reshape(tok_rows, group, head_dim)
        g_grp = grad_out[:, low_col:high_col].reshape(tok_rows, group, head_dim)
        k_grp = all_keys[:, head_group * head_dim : (head_group + 1) * head_dim]
        v_grp = all_values[:, head_group * head_dim : (head_group + 1) * head_dim]
        scores = jnp.einsum("qhd,kd->hqk", q_grp, k_grp, preferred_element_type=jnp.float32) * scale
        sink_col = sinks[head_group * group : (head_group + 1) * group][:, None, None]
        masked = jnp.where(allowed, scores, -jnp.inf)
        peak = jnp.maximum(jnp.max(masked, axis=-1, keepdims=True), sink_col)
        expo = jnp.where(allowed, jnp.exp(masked - peak), 0.0)
        total = jnp.sum(expo, axis=-1, keepdims=True) + jnp.exp(sink_col - peak)
        probs = expo / total
        grad_probs = jnp.einsum("qhd,kd->hqk", g_grp, v_grp, preferred_element_type=jnp.float32)
        delta = jnp.sum(probs * grad_probs, axis=-1, keepdims=True)
        grad_scores = probs * (grad_probs - delta)
        grad_b = grad_scores.astype(jnp.bfloat16)
        grad_q = (
            jnp.einsum("hqk,kd->qhd", grad_b, k_grp, preferred_element_type=jnp.float32) * scale
        )
        query_parts.append(grad_q.reshape(tok_rows, group * head_dim).astype(jnp.bfloat16))
        key_parts.append(
            jnp.einsum("hqk,qhd->kd", grad_b, q_grp, preferred_element_type=jnp.float32) * scale
        )
    grad_query = jnp.concatenate(query_parts, axis=-1)
    key_grads = jnp.concatenate(key_parts, axis=-1)
    back_keys = from_behind(key_grads[:width].astype(jnp.bfloat16), "seq", -1).astype(jnp.float32)
    local_keys = key_grads[width:]
    local_keys = jnp.concatenate(
        [local_keys[: tok_rows - width], local_keys[tok_rows - width :] + back_keys], axis=0
    )
    turned = rotate_back(local_keys.reshape(tok_rows, heads_kv, head_dim), positions)
    k_grads = turned.reshape(tok_rows, heads_kv * head_dim).astype(jnp.bfloat16)
    shard = lax.psum_scatter(
        lax.dot_general(
            layer_input, k_grads, (((0,), (0,)), ((), ())), preferred_element_type=jnp.float32
        ),
        "dp",
        scatter_dimension=0,
        tiled=True,
    )
    shard = lax.psum(shard, "seq")
    return (grad_query[None], shard)


def solution(mesh):
    return jax.shard_map(
        body,
        mesh=mesh,
        in_specs=(
            P("dp", "seq", None),
            P("dp", "seq", None),
            P("dp", "seq", None),
            P("dp", "seq", None),
            P("dp", "seq", None),
            P(),
            P("dp", "seq"),
            P("dp", "seq"),
        ),
        out_specs=(P("dp", "seq", None), P("dp", None)),
        check_vma=False,
    )
```

profile of v0, /device:TPU:0, one launch (start us, length us, event | category | flops | bytes accessed | tf_op | source)
XLA Modules:
  0.0 173.2 jit_solution(16358544082177896071)
XLA Ops:
  7.2 0.8 fusion.83
  8.0 0.6 slice.98
  8.6 2.9 %collective-permute-start.1 = (bf16[128]{0:T(256)(128)(2,1)}, bf16[128]{0:T(256)(128)(2,1)}, u32[]{:S(2)}, u32[]{:S(2)}) collective-permute-start(bf16[128]{0:T(256)(128)(2,1)} %slice.98), channel_id=1, source_target_pairs={{0,1},{1,2},{2,3},{4,5},{5,6},{6,7},{8,9},{9,10},{10,11},{12,13},{... | collective-permute-start | bytes 776 | tf_op jit(solution)/shard_map/ppermute | solution.py:15
  11.5 1.0 copy.35
  12.5 0.6 slice_bitcast_fusion.1
  13.2 4.0 %collective-permute-start = (bf16[128,256]{0,1:T(8,128)(2,1)}, bf16[128,256]{0,1:T(8,128)(2,1)S(1)}, u32[]{:S(2)}, u32[]{:S(2)}) collective-permute-start(bf16[128,256]{0,1:T(8,128)(2,1)} %slice_bitcast_fusion.1), channel_id=1, source_target_pairs={{0,1},{1,2},{2,3},{4,5},{5,6},{6,7},{8,9},{9,10},{10,11},{12,13},{... | collective-permute-start | bytes 196616 | tf_op jit(solution)/shard_map/ppermute | solution.py:15
  17.2 1.0 copy.38
  18.2 0.6 slice_bitcast_fusion
  18.8 1.9 %collective-permute-start.2 = (bf16[128,256]{0,1:T(8,128)(2,1)}, bf16[128,256]{0,1:T(8,128)(2,1)S(1)}, u32[]{:S(2)}, u32[]{:S(2)}) collective-permute-start(bf16[128,256]{0,1:T(8,128)(2,1)} %slice_bitcast_fusion), channel_id=1, source_target_pairs={{0,1},{1,2},{2,3},{4,5},{5,6},{6,7},{8,9},{9,10},{10,11},{12,13},{... | collective-permute-start | bytes 196616 | tf_op jit(solution)/shard_map/ppermute | solution.py:15
  20.7 0.6 negate_power_fusion
  21.3 0.5 iota_add_fusion
  21.9 0.6 fusion.70
  22.4 1.2 convert_element_type.102
  23.7 1.3 fusion.88
  25.0 1.3 fusion.85
  26.3 0.1 copy.48
  26.4 0.1 copy.45
  26.6 0.1 copy.42
  26.7 0.1 copy.37
  26.9 0.9 fusion.86
  27.8 1.1 copy.40
  28.8 1.8 %copy.49 = bf16[256,512]{0,1:T(8,128)(2,1)} copy(bf16[256,512]{1,0:T(8,128)(2,1)} %get-tuple-element.22) | data formatting | bytes 524288 | tf_op jit(solution)/shard_map/slice | solution.py:73
  30.6 1.8 %copy.46 = bf16[256,512]{0,1:T(8,128)(2,1)} copy(bf16[256,512]{1,0:T(8,128)(2,1)} %get-tuple-element.23) | data formatting | bytes 524288 | tf_op jit(solution)/shard_map/slice | solution.py:73
  32.4 0.8 copy.43
  33.3 0.6 convert_element_type.84
  33.9 0.9 fusion.37
  34.8 0.6 fusion.89
  35.4 0.7 fusion.12
  36.1 0.8 fusion.17
  36.9 0.6 fusion.62
  37.5 0.6 fusion.68
  38.1 0.1 exponential_add_fusion.3
  38.1 2.5 %fusion.9 = (f32[8,256]{1,0:T(8,128)S(1)}, f32[8,256]{1,0:T(8,128)S(1)}, f32[8,256]{1,0:T(8,128)S(1)}, f32[8,256]{1,0:T(8,128)S(1)}, f32[384,256,8]{1,0,2:T(8,128)S(1)}) fusion(f32[8,256]{1,0:T(8,128)S(1)} %exponential_add_fusion.3, f32[8,256]{1,0:T(8,128)S(1)} %broadcast_maximum_fusion.3, f32[384,256,8]{1,0,2:T(8,128)S(1)} %get-tuple-element.41, ...), kind=kOutput, calls=%fused_computation.20 | convolution fusion | flops 113336320 | bytes 16334848 | tf_op jit(solution)/shard_map/qhd,kd->hqk/dot_general | solution.py:83
  40.7 2.0 %fusion.11 = (bf16[8,256,384]{1,2,0:T(8,128)(2,1)S(1)}, f32[8,256]{1,0:T(8,128)S(1)}) fusion(f32[384,256,8]{1,0,2:T(8,128)S(1)} %get-tuple-element.42, f32[8,256]{1,0:T(8,128)S(1)} %get-tuple-element.6, f32[8,256]{1,0:T(8,128)S(1)} %exponential_add_fusion.3, f32[8,256]{1,0:T(8,128)S(1)} %broadcast_maximum_fusion.3, f32[384,256,8]{1,0,2:T(8,128)S(1)} %get-tuple-element.41, ...), kind=kLoop, calls=%fused_computation.22 | loop fusion | flops 10221568 | bytes 11149312 | tf_op jit(solution)/shard_map/convert_element_type | solution.py:86
  42.7 0.6 fusion.31
  43.3 0.1 exponential_add_fusion.2
  43.5 2.8 %fusion.6 = (f32[8,256]{1,0:T(8,128)S(1)}, f32[8,256]{1,0:T(8,128)S(1)}, f32[8,256]{1,0:T(8,128)S(1)}, f32[384,256,8]{1,0,2:T(8,128)S(1)}) fusion(f32[8,256]{1,0:T(8,128)S(1)} %exponential_add_fusion.2, f32[8,256]{1,0:T(8,128)S(1)} %broadcast_maximum_fusion.2, f32[384,256,8]{1,0,2:T(8,128)S(1)} %fusion.62, pred[256,384]{0,1:T(8,128)(4,1)S(1)} %fusion.37, ...), kind=kOutput, calls=%fused_computation.14 | convolution fusion | flops 114124800 | bytes 13197312 | tf_op jit(solution)/shard_map/qhd,kd->hqk/dot_general | solution.py:83
  46.3 0.1 exponential_add_fusion
  46.4 0.6 fusion.57
  47.0 0.3 copy-done.10
  47.2 2.2 %fusion.3 = (f32[8,256]{1,0:T(8,128)S(1)}, f32[8,256]{1,0:T(8,128)S(1)}, f32[384,256,8]{1,0,2:T(8,128)S(1)}) fusion(f32[8,256]{1,0:T(8,128)S(1)} %get-tuple-element.46, f32[8,256]{1,0:T(8,128)S(1)} %broadcast_maximum_fusion.1, f32[384,256,8]{1,0,2:T(8,128)S(1)} %fusion.68, pred[256,384]{0,1:T(8,128)(4,1)S(1)} %fusion.37, f32[384,256,8]{1,0,2:T(8,128)S(1)} %fusion.57, ...), kind=kOutput, calls=%fused_computation.8 | convolution fusion | flops 111767552 | bytes 13189120 | tf_op jit(solution)/shard_map/qhd,kd->hqk/dot_general | solution.py:83
  49.5 3.6 %fusion.8 = (bf16[8,256,384]{1,2,0:T(8,128)(2,1)S(1)}, bf16[8,256,384]{1,2,0:T(8,128)(2,1)S(1)}, bf16[8,256,384]{1,2,0:T(8,128)(2,1)S(1)}) fusion(f32[384,256,8]{1,0,2:T(8,128)S(1)} %get-tuple-element.43, f32[8,256]{1,0:T(8,128)S(1)} %get-tuple-element.10, f32[8,256]{1,0:T(8,128)S(1)} %exponential_add_fusion.2, f32[8,256]{1,0:T(8,128)S(1)} %broadcast_maximum_fusion.2, ...), kind=kLoop, calls=%fused_computation.16 | loop fusion | flops 18874368 | bytes 23764992 | tf_op jit(solution)/shard_map/convert_element_type | solution.py:86
  53.2 0.6 fusion.29
  53.8 0.6 fusion.28
  54.4 0.6 fusion.30
  55.0 0.2 copy-done.4
  55.3 1.3 collective-permute-start.3
  56.6 0.2 multiply_cosine_fusion
  56.8 1.6 collective-permute-done.3
  58.5 1.5 convolution_bitcast_fusion
  60.1 3.1 %copy.68 = f32[1536,256]{1,0:T(8,128)} copy(f32[1536,256]{0,1:T(8,128)} %convolution_bitcast_fusion) | data formatting | bytes 3145728
  63.2 0.4 fusion.24
  63.6 0.1 copy.51
  63.7 1.9 %fusion.26 = bf16[64,8,256]{2,0,1:T(8,128)(2,1)S(1)} fusion(bf16[8,256,384]{1,2,0:T(8,128)(2,1)} %copy-done.4, bf16[256,256]{0,1:T(8,128)(2,1)S(1)} %bitcast.210, bf16[128,256]{0,1:T(8,128)(2,1)S(1)} %collective-permute-done), kind=kOutput, calls=%fused_computation.47 | convolution fusion | flops 101023744 | bytes 2031616 | tf_op jit(solution)/shard_map/hqk,kd->qhd/dot_general | solution.py:88
  65.6 0.1 copy.53
  65.8 2.5 %fusion.25 = bf16[64,8,256]{2,0,1:T(8,128)(2,1)} fusion(bf16[8,256,384]{1,2,0:T(8,128)(2,1)} %copy-done.3, bf16[256,256]{0,1:T(8,128)(2,1)S(1)} %bitcast.211, bf16[128,256]{0,1:T(8,128)(2,1)S(1)} %collective-permute-done), kind=kOutput, calls=%fused_computation.46 | convolution fusion | flops 101023744 | bytes 2031616 | tf_op jit(solution)/shard_map/hqk,kd->qhd/dot_general | solution.py:88
  68.3 1.1 copy.52
  69.4 1.2 fusion.27
  70.6 0.1 copy.54
  70.8 60.4 %reduce-scatter.4.cloned.1.call-done = f32[192,256]{1,0:T(8,128)} async-done(((f32[1536,256]{1,0:T(8,128)}), f32[192,256]{1,0:T(8,128)}) %reduce-scatter.4.cloned.1.call-update) | async-done | bytes 196624
  131.2 1.8 %copy.69 = f32[192,256]{0,1:T(8,128)} copy(f32[192,256]{1,0:T(8,128)} %reduce-scatter.4.cloned.1.call-done) | data formatting | bytes 393216
  133.0 1.1 maximum_bitcast_fusion
  134.1 30.6 %all-reduce.2.cloned.1.call-done = f32[192,256]{0,1:T(8,128)} async-done(((f32[192,256]{0,1:T(8,128)}), f32[192,256]{0,1:T(8,128)}) %all-reduce.2.cloned.1.call-update) | async-done | bytes 196624 | tf_op jit(solution)/shard_map/psum | solution.py:111
  164.7 1.7 %copy.59 = f32[192,256]{1,0:T(8,128)} copy(f32[192,256]{0,1:T(8,128)} %all-reduce.2.cloned.1.call-done) | data formatting | bytes 393216
  (47 shorter events, 0.6 us)
Async XLA Ops:
  7.2 51.4 %copy-start = (bf16[1,256,1536]{2,1,0:T(8,128)(2,1)S(1)}, bf16[1,256,1536]{2,1,0:T(8,128)(2,1)}, u32[]{:S(2)}) copy-start(bf16[1,256,1536]{2,1,0:T(8,128)(2,1)} %param.12) | copy-start | bytes 2359300
  7.2 19.7 %copy-start.8 = (bf16[1,256,2048]{2,1,0:T(8,128)(2,1)S(1)}, bf16[1,256,2048]{2,1,0:T(8,128)(2,1)}, u32[]{:S(2)}) copy-start(bf16[1,256,2048]{2,1,0:T(8,128)(2,1)} %param.11) | copy-start | bytes 3145732
  7.2 124.0 %reduce-scatter.4.cloned.1.call-start = ((), (), s32[]{:S(2)}) async-start(), calls=%async_computation.2 | async-start | bytes 1769472
  8.6 24.6 %collective-permute-start.1 = (bf16[128]{0:T(256)(128)(2,1)}, bf16[128]{0:T(256)(128)(2,1)}, u32[]{:S(2)}, u32[]{:S(2)}) collective-permute-start(bf16[128]{0:T(256)(128)(2,1)} %slice.98), channel_id=1, source_target_pairs={{0,1},{1,2},{2,3},{4,5},{5,6},{6,7},{8,9},{9,10},{10,11},{12,13},{... | collective-permute-start | bytes 776 | tf_op jit(solution)/shard_map/ppermute | solution.py:15
  13.2 21.6 %collective-permute-start = (bf16[128,256]{0,1:T(8,128)(2,1)}, bf16[128,256]{0,1:T(8,128)(2,1)S(1)}, u32[]{:S(2)}, u32[]{:S(2)}) collective-permute-start(bf16[128,256]{0,1:T(8,128)(2,1)} %slice_bitcast_fusion.1), channel_id=1, source_target_pairs={{0,1},{1,2},{2,3},{4,5},{5,6},{6,7},{8,9},{9,10},{10,11},{12,13},{... | collective-permute-start | bytes 196616 | tf_op jit(solution)/shard_map/ppermute | solution.py:15
  18.8 19.3 %collective-permute-start.2 = (bf16[128,256]{0,1:T(8,128)(2,1)}, bf16[128,256]{0,1:T(8,128)(2,1)S(1)}, u32[]{:S(2)}, u32[]{:S(2)}) collective-permute-start(bf16[128,256]{0,1:T(8,128)(2,1)} %slice_bitcast_fusion), channel_id=1, source_target_pairs={{0,1},{1,2},{2,3},{4,5},{5,6},{6,7},{8,9},{9,10},{10,11},{12,13},{... | collective-permute-start | bytes 196616 | tf_op jit(solution)/shard_map/ppermute | solution.py:15
  26.4 8.9 %copy-start.5 = (bf16[256,512]{0,1:T(8,128)(2,1)}, bf16[256,512]{0,1:T(8,128)(2,1)S(1)}, u32[]{:S(2)}) copy-start(bf16[256,512]{0,1:T(8,128)(2,1)S(1)} %copy.48) | copy-start | bytes 786436
  34.8 1.3 copy-start.9
  34.8 1.3 copy-start.12
  40.7 2.8 %copy-start.11 = (bf16[256,512]{0,1:T(8,128)(2,1)S(1)}, bf16[256,512]{0,1:T(8,128)(2,1)}, u32[]{:S(2)}) copy-start(bf16[256,512]{0,1:T(8,128)(2,1)} %copy.43) | copy-start | bytes 786436
  43.5 2.9 %copy-start.7 = (bf16[256,512]{0,1:T(8,128)(2,1)S(1)}, bf16[256,512]{0,1:T(8,128)(2,1)}, u32[]{:S(2)}) copy-start(bf16[256,512]{0,1:T(8,128)(2,1)} %copy.49) | copy-start | bytes 786436
  46.3 1.0 copy-start.10
  49.5 4.3 %copy-start.6 = (bf16[256,512]{0,1:T(8,128)(2,1)S(1)}, bf16[256,512]{0,1:T(8,128)(2,1)}, u32[]{:S(2)}) copy-start(bf16[256,512]{0,1:T(8,128)(2,1)} %copy-done.5) | copy-start | bytes 786436
  53.1 1.9 %copy-start.1 = (bf16[8,256,384]{1,2,0:T(8,128)(2,1)}, bf16[8,256,384]{1,2,0:T(8,128)(2,1)S(1)}, u32[]{:S(2)}) copy-start(bf16[8,256,384]{1,2,0:T(8,128)(2,1)S(1)} %get-tuple-element.32) | copy-start | bytes 4718596
  53.1 1.9 %copy-start.3 = (bf16[8,256,384]{1,2,0:T(8,128)(2,1)}, bf16[8,256,384]{1,2,0:T(8,128)(2,1)S(1)}, u32[]{:S(2)}) copy-start(bf16[8,256,384]{1,2,0:T(8,128)(2,1)S(1)} %get-tuple-element.31) | copy-start | bytes 4718596
  53.1 2.1 %copy-start.4 = (bf16[8,256,384]{1,2,0:T(8,128)(2,1)}, bf16[8,256,384]{1,2,0:T(8,128)(2,1)S(1)}, u32[]{:S(2)}) copy-start(bf16[8,256,384]{1,2,0:T(8,128)(2,1)S(1)} %get-tuple-element.33) | copy-start | bytes 4718596
  53.2 3.4 %copy-start.13 = (f32[1,256]{1,0:T(1,128)S(1)}, f32[1,256]{1,0:T(1,128)}, u32[]{:S(2)}) copy-start(f32[1,256]{1,0:T(1,128)} %convert_element_type.102) | copy-start | bytes 3076
  53.2 3.4 %copy-start.14 = (f32[32]{0:T(128)S(1)}, f32[32]{0:T(128)}, u32[]{:S(2)}) copy-start(f32[32]{0:T(128)} %negate_power_fusion) | copy-start | bytes 388
  55.3 3.1 %collective-permute-start.3 = (bf16[128,256]{0,1:T(8,128)(2,1)S(1)}, bf16[128,256]{0,1:T(8,128)(2,1)S(1)}, u32[]{:S(2)}, u32[]{:S(2)}) collective-permute-start(bf16[128,256]{0,1:T(8,128)(2,1)S(1)} %slice.226), channel_id=1, source_target_pairs={{1,0},{2,1},{3,2},{5,4},{6,5},{7,6},{9,8},{10,9},{11,10},{13,12},{... | collective-permute-start | bytes 196616 | tf_op jit(solution)/shard_map/ppermute | solution.py:15
  63.1 101.5 %all-reduce.2.cloned.1.call-start = ((), (), s32[]{:S(2)}) async-start(), calls=%async_computation.1 | async-start | bytes 524288 | tf_op jit(solution)/shard_map/psum | solution.py:111
  63.6 5.8 %copy-start.2 = (bf16[8,256,384]{1,2,0:T(8,128)(2,1)S(1)}, bf16[8,256,384]{1,2,0:T(8,128)(2,1)}, u32[]{:S(2)}) copy-start(bf16[8,256,384]{1,2,0:T(8,128)(2,1)} %copy-done.1) | copy-start | bytes 4718596
Sparse Core Ops, SparseCore 0:
  63.3 67.8 reduce-scatter.3
  133.5 31.1 all-reduce.1
where the time goes:
time: 174 us; the launch traced here: 173 us
  waiting for transfers between devices  92.7 us (53%)
  local copies, waits for them, and re-layouts  22 us (13%)
  matrix products  20.4 us (12%)
  between operations  14.5 us (8%)
  other arithmetic  13.5 us (8%)
  starting transfers between devices  10.2 us (6%)
    unnamed x3, waiting for transfers between devices  60.4 us
    psum x1, waiting for transfers between devices, body(): shard = lax.psum(shard, 'seq')  30.6 us
    ppermute x4, starting transfers between devices, from_behind(): return lax.ppermute(shard, axis, pairs)  10.1 us
    unnamed x35, local copies, waits for them, and re-layouts  9.09 us
    dot_general x4, matrix products, body(): jnp.einsum('qhd,kd->hqk', g_grp, v_grp, preferred_element_type=jnp.float32)  8.07 us
    slice x5, local copies, waits for them, and re-layouts, body(): g_grp = grad_out[:, low_col:high_col].reshape(tok_rows, group, head_dim)  6.38 us
    dot_general x4, matrix products, body(): jnp.einsum('hqk,kd->qhd', grad_b, k_grp, preferred_element_type=jnp.float32)  6.01 us
    convert_element_type x2, other arithmetic, body(): grad_b = grad_scores.astype(jnp.bfloat16)  5.62 us
  transfers between devices with their start and end apart: 6, of which 3 were waited for; matrix products, arithmetic and copies ran while one was open for 17% of the time, Pallas kernels for 0%

commit v1 on v0

--- a/solution.py
+++ b/solution.py
@@ -7,6 +7,11 @@
 WINDOW = 128
 theta_base = 150000.0
 seg_modulus = 256
+
+
+def _put_task(arr):
+    a_next = lax.all_gather(arr, "seq").sum(axis=0)
+    return a_next
 
 
 def from_behind(shard, axis, by):
@@ -108,7 +113,7 @@
         scatter_dimension=0,
         tiled=True,
     )
-    shard = lax.psum(shard, "seq")
+    shard = _put_task(shard)
     return (grad_query[None], shard)
 
 

time: 174 us -> 148 us (0.85)
  waiting for transfers between devices: 92.7 us -> 61 us
  blocking collectives: 0 us -> 8.78 us
  local copies, waits for them, and re-layouts: 22 us -> 18.5 us
    unnamed x3 -> x1, waiting for transfers between devices: 60.4 us -> 0.02 us
    reduce_scatter x0 -> x1, waiting for transfers between devices: none -> 59.4 us  [body(): lax.psum_scatter(lax.dot_general(layer_input, k_grads, (((0,), (0,)), (()...]
    psum x1 -> x0, waiting for transfers between devices: 30.6 us -> none  [body(): shard = lax.psum(shard, 'seq')]
    all_gather x0 -> x1, blocking collectives: none -> 8.78 us  [_put_task(): a_next = lax.all_gather(arr, 'seq').sum(axis=0)]
    unnamed x35 -> x33, local copies, waits for them, and re-layouts: 9.09 us -> 5.59 us
  transfers between devices with their start and end apart: 6 -> 5, of which waited for: 3 -> 2; matrix products, arithmetic and copies ran while one was open for 17% -> 20% of each run, Pallas kernels for 0% -> 0%
where the time goes in v1:
time: 148 us
  waiting for transfers between devices  61 us (41%)
  matrix products  20.4 us (14%)
  local copies, waits for them, and re-layouts  18.5 us (12%)
  between operations  14.5 us (10%)
  other arithmetic  14.3 us (10%)
  starting transfers between devices  10.2 us (7%)
  blocking collectives  8.78 us (6%)
    reduce_scatter x1, waiting for transfers between devices, body(): lax.psum_scatter(lax.dot_general(layer_input, k_grads, (((0,), (0,)), (()...  59.4 us
    ppermute x4, starting transfers between devices, from_behind(): return lax.ppermute(shard, axis, pairs)  10.1 us
    all_gather x1, blocking collectives, _put_task(): a_next = lax.all_gather(arr, 'seq').sum(axis=0)  8.78 us
    dot_general x4, matrix products, body(): jnp.einsum('qhd,kd->hqk', g_grp, v_grp, preferred_element_type=jnp.float32)  8.07 us
    slice x5, local copies, waits for them, and re-layouts, body(): g_grp = grad_out[:, low_col:high_col].reshape(tok_rows, group, head_dim)  6.38 us
    dot_general x4, matrix products, body(): jnp.einsum('hqk,kd->qhd', grad_b, k_grp, preferred_element_type=jnp.float32)  6.01 us
    convert_element_type x2, other arithmetic, body(): grad_b = grad_scores.astype(jnp.bfloat16)  5.62 us
    unnamed x33, local copies, waits for them, and re-layouts  5.59 us
  transfers between devices with their start and end apart: 5, of which 2 were waited for; matrix products, arithmetic and copies ran while one was open for 20% of the time, Pallas kernels for 0%

profile of v1, /device:TPU:0, one launch (start us, length us, event | category | flops | bytes accessed | tf_op | source)
XLA Modules:
  0.0 147.5 jit_solution(1178555032579489738)
XLA Ops:
  7.2 0.8 fusion.83
  8.0 0.6 slice.98
  8.6 2.9 %collective-permute-start.1 = (bf16[128]{0:T(256)(128)(2,1)}, bf16[128]{0:T(256)(128)(2,1)}, u32[]{:S(2)}, u32[]{:S(2)}) collective-permute-start(bf16[128]{0:T(256)(128)(2,1)} %slice.98), channel_id=1, source_target_pairs={{0,1},{1,2},{2,3},{4,5},{5,6},{6,7},{8,9},{9,10},{10,11},{12,13},{... | collective-permute-start | bytes 776 | tf_op jit(solution)/shard_map/ppermute | solution.py:20
  11.5 1.0 copy.59
  12.5 0.6 slice_bitcast_fusion.1
  13.2 4.0 %collective-permute-start = (bf16[128,256]{0,1:T(8,128)(2,1)}, bf16[128,256]{0,1:T(8,128)(2,1)S(1)}, u32[]{:S(2)}, u32[]{:S(2)}) collective-permute-start(bf16[128,256]{0,1:T(8,128)(2,1)} %slice_bitcast_fusion.1), channel_id=1, source_target_pairs={{0,1},{1,2},{2,3},{4,5},{5,6},{6,7},{8,9},{9,10},{10,11},{12,13},{... | collective-permute-start | bytes 196616 | tf_op jit(solution)/shard_map/ppermute | solution.py:20
  17.2 1.0 copy.62
  18.2 0.6 slice_bitcast_fusion
  18.8 1.9 %collective-permute-start.2 = (bf16[128,256]{0,1:T(8,128)(2,1)}, bf16[128,256]{0,1:T(8,128)(2,1)S(1)}, u32[]{:S(2)}, u32[]{:S(2)}) collective-permute-start(bf16[128,256]{0,1:T(8,128)(2,1)} %slice_bitcast_fusion), channel_id=1, source_target_pairs={{0,1},{1,2},{2,3},{4,5},{5,6},{6,7},{8,9},{9,10},{10,11},{12,13},{... | collective-permute-start | bytes 196616 | tf_op jit(solution)/shard_map/ppermute | solution.py:20
  20.7 0.6 negate_power_fusion
  21.3 0.5 iota_add_fusion
  21.9 0.6 fusion.70
  22.4 1.2 convert_element_type.102
  23.7 1.3 fusion.88
  25.0 1.3 fusion.85
  26.3 0.1 copy.72
  26.4 0.1 copy.69
  26.6 0.1 copy.66
  26.7 0.1 copy.61
  26.9 0.9 fusion.86
  27.8 1.1 copy.64
  28.8 1.8 %copy.73 = bf16[256,512]{0,1:T(8,128)(2,1)} copy(bf16[256,512]{1,0:T(8,128)(2,1)} %get-tuple-element.18) | data formatting | bytes 524288 | tf_op jit(solution)/shard_map/slice | solution.py:78
  30.6 1.8 %copy.70 = bf16[256,512]{0,1:T(8,128)(2,1)} copy(bf16[256,512]{1,0:T(8,128)(2,1)} %get-tuple-element.19) | data formatting | bytes 524288 | tf_op jit(solution)/shard_map/slice | solution.py:78
  32.4 0.8 copy.67
  33.3 0.6 convert_element_type.84
  33.9 0.9 fusion.37
  34.8 0.6 fusion.89
  35.4 0.7 fusion.12
  36.0 0.1 broadcast_maximum_fusion.3
  36.1 0.8 fusion.17
  36.9 0.6 fusion.62
  37.5 0.6 fusion.68
  38.1 0.1 exponential_add_fusion.3
  38.1 2.5 %fusion.9 = (f32[8,256]{1,0:T(8,128)S(1)}, f32[8,256]{1,0:T(8,128)S(1)}, f32[8,256]{1,0:T(8,128)S(1)}, f32[8,256]{1,0:T(8,128)S(1)}, f32[384,256,8]{1,0,2:T(8,128)S(1)}) fusion(f32[8,256]{1,0:T(8,128)S(1)} %exponential_add_fusion.3, f32[8,256]{1,0:T(8,128)S(1)} %broadcast_maximum_fusion.3, f32[384,256,8]{1,0,2:T(8,128)S(1)} %get-tuple-element.37, ...), kind=kOutput, calls=%fused_computation.20 | convolution fusion | flops 113336320 | bytes 16334848 | tf_op jit(solution)/shard_map/qhd,kd->hqk/dot_general | solution.py:88
  40.7 2.0 %fusion.11 = (bf16[8,256,384]{1,2,0:T(8,128)(2,1)S(1)}, f32[8,256]{1,0:T(8,128)S(1)}) fusion(f32[384,256,8]{1,0,2:T(8,128)S(1)} %get-tuple-element.38, f32[8,256]{1,0:T(8,128)S(1)} %get-tuple-element.2, f32[8,256]{1,0:T(8,128)S(1)} %exponential_add_fusion.3, f32[8,256]{1,0:T(8,128)S(1)} %broadcast_maximum_fusion.3, f32[384,256,8]{1,0,2:T(8,128)S(1)} %get-tuple-element.37, ...), kind=kLoop, calls=%fused_computation.22 | loop fusion | flops 10221568 | bytes 11149312 | tf_op jit(solution)/shard_map/convert_element_type | solution.py:91
  42.7 0.6 fusion.31
  43.3 0.1 exponential_add_fusion.2
  43.5 2.8 %fusion.6 = (f32[8,256]{1,0:T(8,128)S(1)}, f32[8,256]{1,0:T(8,128)S(1)}, f32[8,256]{1,0:T(8,128)S(1)}, f32[384,256,8]{1,0,2:T(8,128)S(1)}) fusion(f32[8,256]{1,0:T(8,128)S(1)} %exponential_add_fusion.2, f32[8,256]{1,0:T(8,128)S(1)} %broadcast_maximum_fusion.2, f32[384,256,8]{1,0,2:T(8,128)S(1)} %fusion.62, pred[256,384]{0,1:T(8,128)(4,1)S(1)} %fusion.37, ...), kind=kOutput, calls=%fused_computation.14 | convolution fusion | flops 114124800 | bytes 13197312 | tf_op jit(solution)/shard_map/qhd,kd->hqk/dot_general | solution.py:88
  46.3 0.1 exponential_add_fusion
  46.4 0.6 fusion.57
  47.0 0.3 copy-done.10
  47.2 2.2 %fusion.3 = (f32[8,256]{1,0:T(8,128)S(1)}, f32[8,256]{1,0:T(8,128)S(1)}, f32[384,256,8]{1,0,2:T(8,128)S(1)}) fusion(f32[8,256]{1,0:T(8,128)S(1)} %get-tuple-element.42, f32[8,256]{1,0:T(8,128)S(1)} %broadcast_maximum_fusion.1, f32[384,256,8]{1,0,2:T(8,128)S(1)} %fusion.68, pred[256,384]{0,1:T(8,128)(4,1)S(1)} %fusion.37, f32[384,256,8]{1,0,2:T(8,128)S(1)} %fusion.57, ...), kind=kOutput, calls=%fused_computation.8 | convolution fusion | flops 111767552 | bytes 13189120 | tf_op jit(solution)/shard_map/qhd,kd->hqk/dot_general | solution.py:88
  49.5 3.6 %fusion.8 = (bf16[8,256,384]{1,2,0:T(8,128)(2,1)S(1)}, bf16[8,256,384]{1,2,0:T(8,128)(2,1)S(1)}, bf16[8,256,384]{1,2,0:T(8,128)(2,1)S(1)}) fusion(f32[384,256,8]{1,0,2:T(8,128)S(1)} %get-tuple-element.39, f32[8,256]{1,0:T(8,128)S(1)} %get-tuple-element.6, f32[8,256]{1,0:T(8,128)S(1)} %exponential_add_fusion.2, f32[8,256]{1,0:T(8,128)S(1)} %broadcast_maximum_fusion.2, ...), kind=kLoop, calls=%fused_computation.16 | loop fusion | flops 18874368 | bytes 23764992 | tf_op jit(solution)/shard_map/convert_element_type | solution.py:91
  53.2 0.6 fusion.29
  53.8 0.6 fusion.28
  54.4 0.6 fusion.30
  55.0 0.2 copy-done.4
  55.3 1.3 collective-permute-start.3
  56.6 0.2 multiply_cosine_fusion
  56.8 1.6 %collective-permute-done.3 = bf16[128,256]{0,1:T(8,128)(2,1)S(1)} collective-permute-done((bf16[128,256]{0,1:T(8,128)(2,1)S(1)}, bf16[128,256]{0,1:T(8,128)(2,1)S(1)}, u32[]{:S(2)}, u32[]{:S(2)}) %collective-permute-start.3) | collective-permute-done | bytes 65568 | tf_op jit(solution)/shard_map/ppermute | solution.py:20
  58.5 1.5 %convolution_bitcast_fusion = f32[1536,256]{0,1:T(8,128)} fusion(bf16[256,256]{0,1:T(8,128)(2,1)S(1)} %bitcast.234, bf16[1,256,1536]{2,1,0:T(8,128)(2,1)S(1)} %copy-done), kind=kOutput, calls=%fused_computation.32 | convolution fusion | flops 201326592 | bytes 2490368 | tf_op jit(solution)/shard_map/dot_general | solution.py:109
  60.1 3.1 %copy.92 = f32[1536,256]{1,0:T(8,128)} copy(f32[1536,256]{0,1:T(8,128)} %convolution_bitcast_fusion) | data formatting | bytes 3145728
  63.1 0.4 fusion.24
  63.6 0.1 copy.75
  63.7 1.9 %fusion.26 = bf16[64,8,256]{2,0,1:T(8,128)(2,1)S(1)} fusion(bf16[8,256,384]{1,2,0:T(8,128)(2,1)} %copy-done.4, bf16[256,256]{0,1:T(8,128)(2,1)S(1)} %bitcast.211, bf16[128,256]{0,1:T(8,128)(2,1)S(1)} %collective-permute-done), kind=kOutput, calls=%fused_computation.47 | convolution fusion | flops 101023744 | bytes 2031616 | tf_op jit(solution)/shard_map/hqk,kd->qhd/dot_general | solution.py:93
  65.6 0.1 copy.77
  65.7 2.5 %fusion.25 = bf16[64,8,256]{2,0,1:T(8,128)(2,1)} fusion(bf16[8,256,384]{1,2,0:T(8,128)(2,1)} %copy-done.3, bf16[256,256]{0,1:T(8,128)(2,1)S(1)} %bitcast.212, bf16[128,256]{0,1:T(8,128)(2,1)S(1)} %collective-permute-done), kind=kOutput, calls=%fused_computation.46 | convolution fusion | flops 101023744 | bytes 2031616 | tf_op jit(solution)/shard_map/hqk,kd->qhd/dot_general | solution.py:93
  68.3 1.1 copy.76
  69.4 1.2 fusion.27
  70.6 0.1 copy.78
  70.7 1.1 maximum_bitcast_fusion
  71.8 59.4 %reduce-scatter.4.cloned.1.call-done = f32[192,256]{1,0:T(8,128)} async-done(((f32[1536,256]{1,0:T(8,128)}), f32[192,256]{1,0:T(8,128)}) %reduce-scatter.4.cloned.1.call-update) | async-done | bytes 196624 | tf_op jit(solution)/shard_map/reduce_scatter | solution.py:108
  131.2 8.8 %all-gather = f32[768,256]{1,0:T(8,128)S(1)} all-gather(f32[192,256]{1,0:T(8,128)} %reduce-scatter.4.cloned.1.call-done), channel_id=2, replica_groups=mesh['dp'=8,'seq'=4] {'seq'}, dimensions={0}, use_global_device_ids=true | all-gather | bytes 983040 | tf_op jit(solution)/shard_map/all_gather | solution.py:13
  140.0 0.7 reduce_sum.89
  (44 shorter events, 0.5 us)
Async XLA Ops:
  7.2 51.4 %copy-start = (bf16[1,256,1536]{2,1,0:T(8,128)(2,1)S(1)}, bf16[1,256,1536]{2,1,0:T(8,128)(2,1)}, u32[]{:S(2)}) copy-start(bf16[1,256,1536]{2,1,0:T(8,128)(2,1)} %param.12) | copy-start | bytes 2359300
  7.2 19.7 %copy-start.8 = (bf16[1,256,2048]{2,1,0:T(8,128)(2,1)S(1)}, bf16[1,256,2048]{2,1,0:T(8,128)(2,1)}, u32[]{:S(2)}) copy-start(bf16[1,256,2048]{2,1,0:T(8,128)(2,1)} %param.11) | copy-start | bytes 3145732
  7.2 124.0 %reduce-scatter.4.cloned.1.call-start = ((), (), s32[]{:S(2)}) async-start(), calls=%async_computation.1 | async-start | bytes 1769472 | tf_op jit(solution)/shard_map/reduce_scatter | solution.py:108
  8.6 24.6 %collective-permute-start.1 = (bf16[128]{0:T(256)(128)(2,1)}, bf16[128]{0:T(256)(128)(2,1)}, u32[]{:S(2)}, u32[]{:S(2)}) collective-permute-start(bf16[128]{0:T(256)(128)(2,1)} %slice.98), channel_id=1, source_target_pairs={{0,1},{1,2},{2,3},{4,5},{5,6},{6,7},{8,9},{9,10},{10,11},{12,13},{... | collective-permute-start | bytes 776 | tf_op jit(solution)/shard_map/ppermute | solution.py:20
  13.2 21.6 %collective-permute-start = (bf16[128,256]{0,1:T(8,128)(2,1)}, bf16[128,256]{0,1:T(8,128)(2,1)S(1)}, u32[]{:S(2)}, u32[]{:S(2)}) collective-permute-start(bf16[128,256]{0,1:T(8,128)(2,1)} %slice_bitcast_fusion.1), channel_id=1, source_target_pairs={{0,1},{1,2},{2,3},{4,5},{5,6},{6,7},{8,9},{9,10},{10,11},{12,13},{... | collective-permute-start | bytes 196616 | tf_op jit(solution)/shard_map/ppermute | solution.py:20
  18.8 19.3 %collective-permute-start.2 = (bf16[128,256]{0,1:T(8,128)(2,1)}, bf16[128,256]{0,1:T(8,128)(2,1)S(1)}, u32[]{:S(2)}, u32[]{:S(2)}) collective-permute-start(bf16[128,256]{0,1:T(8,128)(2,1)} %slice_bitcast_fusion), channel_id=1, source_target_pairs={{0,1},{1,2},{2,3},{4,5},{5,6},{6,7},{8,9},{9,10},{10,11},{12,13},{... | collective-permute-start | bytes 196616 | tf_op jit(solution)/shard_map/ppermute | solution.py:20
  26.4 8.9 %copy-start.5 = (bf16[256,512]{0,1:T(8,128)(2,1)}, bf16[256,512]{0,1:T(8,128)(2,1)S(1)}, u32[]{:S(2)}) copy-start(bf16[256,512]{0,1:T(8,128)(2,1)S(1)} %copy.72) | copy-start | bytes 786436
  34.8 1.3 copy-start.9
  34.8 1.3 copy-start.12
  40.7 2.8 %copy-start.11 = (bf16[256,512]{0,1:T(8,128)(2,1)S(1)}, bf16[256,512]{0,1:T(8,128)(2,1)}, u32[]{:S(2)}) copy-start(bf16[256,512]{0,1:T(8,128)(2,1)} %copy.67) | copy-start | bytes 786436
  43.5 2.9 %copy-start.7 = (bf16[256,512]{0,1:T(8,128)(2,1)S(1)}, bf16[256,512]{0,1:T(8,128)(2,1)}, u32[]{:S(2)}) copy-start(bf16[256,512]{0,1:T(8,128)(2,1)} %copy.73) | copy-start | bytes 786436
  46.3 1.0 copy-start.10
  49.5 4.3 %copy-start.6 = (bf16[256,512]{0,1:T(8,128)(2,1)S(1)}, bf16[256,512]{0,1:T(8,128)(2,1)}, u32[]{:S(2)}) copy-start(bf16[256,512]{0,1:T(8,128)(2,1)} %copy-done.5) | copy-start | bytes 786436
  53.1 1.9 %copy-start.1 = (bf16[8,256,384]{1,2,0:T(8,128)(2,1)}, bf16[8,256,384]{1,2,0:T(8,128)(2,1)S(1)}, u32[]{:S(2)}) copy-start(bf16[8,256,384]{1,2,0:T(8,128)(2,1)S(1)} %get-tuple-element.28) | copy-start | bytes 4718596
  53.1 1.9 %copy-start.3 = (bf16[8,256,384]{1,2,0:T(8,128)(2,1)}, bf16[8,256,384]{1,2,0:T(8,128)(2,1)S(1)}, u32[]{:S(2)}) copy-start(bf16[8,256,384]{1,2,0:T(8,128)(2,1)S(1)} %get-tuple-element.27) | copy-start | bytes 4718596
  53.1 2.1 %copy-start.4 = (bf16[8,256,384]{1,2,0:T(8,128)(2,1)}, bf16[8,256,384]{1,2,0:T(8,128)(2,1)S(1)}, u32[]{:S(2)}) copy-start(bf16[8,256,384]{1,2,0:T(8,128)(2,1)S(1)} %get-tuple-element.29) | copy-start | bytes 4718596
  53.2 3.4 %copy-start.13 = (f32[1,256]{1,0:T(1,128)S(1)}, f32[1,256]{1,0:T(1,128)}, u32[]{:S(2)}) copy-start(f32[1,256]{1,0:T(1,128)} %convert_element_type.102) | copy-start | bytes 3076
  53.2 3.4 %copy-start.14 = (f32[32]{0:T(128)S(1)}, f32[32]{0:T(128)}, u32[]{:S(2)}) copy-start(f32[32]{0:T(128)} %negate_power_fusion) | copy-start | bytes 388
  55.3 3.1 %collective-permute-start.3 = (bf16[128,256]{0,1:T(8,128)(2,1)S(1)}, bf16[128,256]{0,1:T(8,128)(2,1)S(1)}, u32[]{:S(2)}, u32[]{:S(2)}) collective-permute-start(bf16[128,256]{0,1:T(8,128)(2,1)S(1)} %slice.226), channel_id=1, source_target_pairs={{1,0},{2,1},{3,2},{5,4},{6,5},{7,6},{9,8},{10,9},{11,10},{13,12},{... | collective-permute-start | bytes 196616 | tf_op jit(solution)/shard_map/ppermute | solution.py:20
  63.5 5.8 %copy-start.2 = (bf16[8,256,384]{1,2,0:T(8,128)(2,1)S(1)}, bf16[8,256,384]{1,2,0:T(8,128)(2,1)}, u32[]{:S(2)}) copy-start(bf16[8,256,384]{1,2,0:T(8,128)(2,1)} %copy-done.1) | copy-start | bytes 4718596
Sparse Core Ops, SparseCore 0:
  63.3 67.8 reduce-scatter.3
